TPU v7x, 256 devices: a whole 4x4x8 slice. The times are simulated.
256 devices in a mesh: rows: 8 (over x, core), protos: 32 (over y, z).
Axes of the slice: x: 4, y: 4, z: 8, core: 2. Of those that a mesh axis runs over, the one named last changes fastest.
Arguments:
- teacher_features: bfloat16 [4096, 384], P(('rows', 'protos')), may hold values from -80 to 80, as said below
- student_features: bfloat16 [4096, 384], P(('rows', 'protos')), may hold values from -80 to 80, as said below
- prototypes: bfloat16 [131072, 384], P('protos'), may hold values from -80 to 80, as said below
Outputs:
- feature_grad: float32 [4096, 384], P(('rows', 'protos'))
- proto_grad: float32 [8, 16384, 384], P('rows', 'protos')
Inputs may be any that keep to these rules, and one draw needn't show every extreme that they name: `teacher_features`: every row has nonzero entries. `student_features`: every row has nonzero entries. `prototypes`: every row has nonzero entries.
All inputs are finite; a program needn't handle non-finite values.
Results may differ from a plain program's by a relative error of at most 0.012.
The roundings to bfloat16 on the way count: a program that leaves them out, or rounds other values in their place, can miss the bound.
Values may be sent and summed in bfloat16 or wider, within the bound.
A program may use at most 64 MiB of HBM per device.

v0:
```python
import math
import jax
import jax.numpy as jnp
from jax import lax
from jax.sharding import PartitionSpec as P

D = 384
K = 131072
PASSES = 3
eps = 1e-06


def unitize(values):
    values = values.astype(jnp.float32)
    return (values * lax.rsqrt(jnp.sum(values * values, axis=1, keepdims=True) + eps)).astype(
        jnp.bfloat16
    )


def against(left, right):
    return lax.dot_general(
        left, right, (((1,), (1,)), ((), ())), preferred_element_type=jnp.float32
    )


def on_device(teacher_features, student_features, prototypes):
    scale = 1.5 * math.sqrt(D)
    unit_w = unitize(prototypes)
    local_t = unitize(teacher_features)
    local_s = unitize(student_features)
    unit_t, unit_s = (
        lax.all_gather(local_t, "protos", axis=0, tiled=True),
        lax.all_gather(local_s, "protos", axis=0, tiled=True),
    )
    kernel = jnp.exp(scale * against(unit_t, unit_w))
    powers = jnp.exp(scale * against(unit_s, unit_w))
    student_part = jnp.sum(powers, axis=1)
    student_whole = lax.psum(student_part, "protos")
    row_scale = jnp.ones((kernel.shape[0],), jnp.float32)
    col_scale = jnp.ones((kernel.shape[1],), jnp.float32)
    for step in range(PASSES):
        col_part = jnp.dot(row_scale, kernel, precision=lax.Precision.HIGHEST)
        col_scale = 1.0 / lax.psum(col_part, "rows")
        row_part = jnp.dot(kernel, col_scale, precision=lax.Precision.HIGHEST)
        if step == 0:
            row_whole = lax.psum(row_part, "protos")
        else:
            row_whole = lax.psum(row_part, "protos")
        row_scale = 1.0 / row_whole
    target = kernel * row_scale[:, None] * col_scale[None, :]
    probs = powers / student_whole[:, None]
    delta = (probs - target).astype(jnp.bfloat16)
    feature_term = scale * jnp.dot(delta, unit_w, preferred_element_type=jnp.float32)
    feature_grad = lax.psum_scatter(feature_term, "protos", scatter_dimension=0, tiled=True)
    row_groups = lax.axis_size("rows")
    total_rows = delta.shape[0] * row_groups
    factor = scale * K / total_rows
    block = delta.shape[1] // row_groups
    term = factor * lax.dot_general(
        delta, unit_s, (((0,), (0,)), ((), ())), preferred_element_type=jnp.float32
    )
    proto_grad = lax.psum_scatter(
        term.reshape(row_groups, block, term.shape[1]), "rows", scatter_dimension=0, tiled=True
    )
    return (feature_grad, proto_grad)


def solution(mesh):
    return jax.shard_map(
        on_device,
        mesh=mesh,
        in_specs=(P(("rows", "protos"), None), P(("rows", "protos"), None), P("protos", None)),
        out_specs=(P(("rows", "protos"), None), P("rows", "protos", None)),
        check_vma=False,
    )
```

profile of v0, /device:TPU:1, one launch (start us, length us, event | category | flops | bytes accessed | tf_op | source)
XLA Modules:
  0.0 735.6 jit_solution(5828482277272511359)
XLA Ops:
  7.2 0.0 reduce-scatter.3.cloned.1.call-start
  7.2 0.8 fusion.5
  8.0 0.8 fusion.3
  8.9 0.8 fusion.4
  9.7 0.8 fusion.6
  10.4 2.6 fusion.1
  13.0 0.0 copy-start.3
  13.1 41.6 %all_gather.6 = bf16[512,384]{1,0:T(8,128)(2,1)S(1)} all-gather(bf16[16,384]{1,0:T(8,128)(2,1)S(1)} %fusion.4), channel_id=1, replica_groups=mesh['rows'=8,'protos'=32] {'protos'}, dimensions={0}, use_global_device_ids=true | all-gather | bytes 405504 | tf_op jit(solution)/shard_map/all_gather | solution.py:33
  54.6 36.7 %all_gather.7 = bf16[512,384]{1,0:T(8,128)(2,1)S(1)} all-gather(bf16[16,384]{1,0:T(8,128)(2,1)S(1)} %fusion.6), channel_id=1, replica_groups=mesh['rows'=8,'protos'=32] {'protos'}, dimensions={0}, use_global_device_ids=true | all-gather | bytes 405504 | tf_op jit(solution)/shard_map/all_gather | solution.py:32
  91.3 4.3 multiply_exponential_fusion
  95.7 0.0 copy-start
  95.7 3.2 copy-done
  98.9 4.0 fusion.7
  102.9 0.0 copy-done.3
  102.9 44.7 %psum.50 = f32[4096]{0:T(1024)S(1)} all-reduce(f32[4096]{0:T(1024)S(1)} %bitcast.34), channel_id=1, replica_groups=mesh['rows'=8,'protos'=32] {'rows'}, use_global_device_ids=true, to_apply=%region_5.0 | all-reduce | flops 4096 | bytes 32768 | tf_op jit(solution)/shard_map/psum | solution.py:43
  147.7 9.4 %fusion.14 = f32[1,512]{1,0:T(1,128)S(1)} fusion(f32[512,4096]{1,0:T(8,128)} %copy-done, f32[4096,1]{0,1:T(1,128)S(1)} %bitcast.30), kind=kOutput, calls=%fused_computation.31 | convolution fusion | flops 25165824 | bytes 8407040 | tf_op jit(solution)/shard_map/dot_general | solution.py:44
  157.1 58.6 %psum.51 = f32[512]{0:T(512)S(1)} all-reduce(f32[512]{0:T(512)S(1)} %bitcast.36), channel_id=1, replica_groups=mesh['rows'=8,'protos'=32] {'protos'}, use_global_device_ids=true, to_apply=%region_6.0 | all-reduce | flops 512 | bytes 4096 | tf_op jit(solution)/shard_map/psum | solution.py:46
  215.7 6.3 fusion.15
  222.1 37.4 %psum.52 = f32[4096]{0:T(1024)S(1)} all-reduce(f32[4096]{0:T(1024)S(1)} %bitcast.31), channel_id=1, replica_groups=mesh['rows'=8,'protos'=32] {'rows'}, use_global_device_ids=true, to_apply=%region_7.0 | all-reduce | flops 4096 | bytes 32768 | tf_op jit(solution)/shard_map/psum | solution.py:43
  259.5 9.4 %fusion.16 = f32[1,512]{1,0:T(1,128)S(1)} fusion(f32[512,4096]{1,0:T(8,128)} %copy-done, f32[4096,1]{0,1:T(1,128)S(1)} %bitcast.32), kind=kOutput, calls=%fused_computation.33 | convolution fusion | flops 25165824 | bytes 8407040 | tf_op jit(solution)/shard_map/dot_general | solution.py:44
  268.9 55.8 %psum.53 = f32[512]{0:T(512)S(1)} all-reduce(f32[512]{0:T(512)S(1)} %bitcast.38), channel_id=1, replica_groups=mesh['rows'=8,'protos'=32] {'protos'}, use_global_device_ids=true, to_apply=%region_8.0 | all-reduce | flops 512 | bytes 4096 | tf_op jit(solution)/shard_map/psum | solution.py:48
  324.7 0.0 copy-start.1
  324.7 6.5 fusion.17
  331.2 37.6 %psum.54 = f32[4096]{0:T(1024)} all-reduce(f32[4096]{0:T(1024)S(1)} %bitcast.33), channel_id=1, replica_groups=mesh['rows'=8,'protos'=32] {'rows'}, use_global_device_ids=true, to_apply=%region_9.0 | all-reduce | flops 4096 | bytes 32768 | tf_op jit(solution)/shard_map/psum | solution.py:43
  368.8 0.7 broadcast_divide_fusion
  369.6 10.0 %fusion.18 = f32[1,512]{1,0:T(1,128)} fusion(f32[512,4096]{1,0:T(8,128)} %copy-done, f32[4096,1]{0,1:T(1,128)S(1)} %bitcast.29), kind=kOutput, calls=%fused_computation.35 | convolution fusion | flops 25165824 | bytes 8407040 | tf_op jit(solution)/shard_map/dot_general | solution.py:44
  379.6 0.0 copy-done.1
  379.6 6.2 fusion
  385.8 58.2 %all-reduce = (f32[512]{0:T(512)}, f32[512]{0:T(512)}) all-reduce(f32[512]{0:T(512)} %bitcast.35, f32[512]{0:T(512)} %get-tuple-element.4), channel_id=1, replica_groups=mesh['rows'=8,'protos'=32] {'protos'}, use_global_device_ids=true, to_apply=%region_10.0 | all-reduce | flops 1024 | bytes 8192 | tf_op jit(solution)/shard_map/psum | solution.py:48
  444.0 0.7 broadcast_divide_fusion.5
  444.6 0.0 copy-start.4
  444.6 7.3 subtract_convert_fusion
  452.0 0.0 copy-start.2
  452.0 2.0 copy-done.2
  454.0 0.0 copy-done.4
  454.0 3.3 convolution_multiply_fusion.1
  457.4 0.0 reduce-scatter.3.cloned.1.call-update
  457.4 0.0 reduce-scatter.5.cloned.1.call-start
  457.4 7.2 convolution_multiply_fusion
  464.7 0.0 reduce-scatter.5.cloned.1.call-update
  464.7 212.9 %reduce-scatter.3.cloned.1.call-done = f32[16,384]{1,0:T(8,128)} async-done(((f32[512,384]{1,0:T(8,128)}), f32[16,384]{1,0:T(8,128)}) %reduce-scatter.3.cloned.1.call-update) | async-done | bytes 24592 | tf_op jit(solution)/shard_map/reduce_scatter | solution.py:54
  677.6 51.2 %reduce-scatter.5.cloned.1.call-done = f32[1,512,384]{2,1,0:T(8,128)} async-done(((f32[8,512,384]{2,1,0:T(8,128)}), f32[1,512,384]{2,1,0:T(8,128)}) %reduce-scatter.5.cloned.1.call-update) | async-done | bytes 786448 | tf_op jit(solution)/shard_map/reduce_scatter | solution.py:62
  (7 shorter events, 0.0 us)
Async XLA Ops:
  7.2 670.4 %reduce-scatter.3.cloned.1.call-start = ((), (), s32[]{:S(2)}) async-start(), calls=%async_computation.2 | async-start | bytes 811008 | tf_op jit(solution)/shard_map/reduce_scatter | solution.py:54
  13.0 89.9 %copy-start.3 = (f32[4096]{0:T(1024)}, f32[4096]{0:T(1024)S(1)}, u32[]{:S(2)}) copy-start(f32[4096]{0:T(1024)S(1)} %add_rsqrt_fusion) | copy-start | bytes 49156
  95.7 3.2 copy-start
  324.7 54.9 %copy-start.1 = (bf16[4096,384]{1,0:T(8,128)(2,1)S(1)}, bf16[4096,384]{1,0:T(8,128)(2,1)}, u32[]{:S(2)}) copy-start(bf16[4096,384]{1,0:T(8,128)(2,1)} %param.5) | copy-start | bytes 9437188
  444.6 9.4 %copy-start.4 = (f32[4096]{0:T(1024)S(1)}, f32[4096]{0:T(1024)}, u32[]{:S(2)}) copy-start(f32[4096]{0:T(1024)} %copy-done.3) | copy-start | bytes 49156
  452.0 2.0 copy-start.2
  457.4 271.4 %reduce-scatter.5.cloned.1.call-start = ((), (), s32[]{:S(2)}) async-start(), calls=%async_computation.3 | async-start | bytes 7077888 | tf_op jit(solution)/shard_map/reduce_scatter | solution.py:62
Sparse Core Ops, SparseCore 0:
  457.5 220.0 reduce-scatter.2
  680.7 48.0 reduce-scatter.4
where the time goes:
time: 736 us
  blocking collectives  371 us (50%)
  waiting for transfers between devices  264 us (36%)
  matrix products  66.9 us (9%)
  other arithmetic  14.6 us (2%)
  between operations  14.1 us (2%)
    reduce_scatter x1, waiting for transfers between devices, on_device(): lax.psum_scatter(feature_term, 'protos', scatter_dimension=0, tiled=True)  213 us
    psum x3, blocking collectives, on_device(): row_whole = lax.psum(row_part, 'protos')  173 us
    psum x3, blocking collectives, on_device(): col_scale = 1.0 / lax.psum(col_part, 'rows')  120 us
    reduce_scatter x1, waiting for transfers between devices, on_device(): lax.psum_scatter(term.reshape(row_groups, block, term.shape[1]), 'rows',...  51.2 us
    all_gather x1, blocking collectives, on_device(): lax.all_gather(local_s, 'protos', axis=0, tiled=True)  41.6 us
    all_gather x1, blocking collectives, on_device(): lax.all_gather(local_t, 'protos', axis=0, tiled=True)  36.7 us
    dot_general x3, matrix products, on_device(): row_part = jnp.dot(kernel, col_scale, precision=lax.Precision.HIGHEST)  28.9 us
    dot_general x3, matrix products, on_device(): col_part = jnp.dot(row_scale, kernel, precision=lax.Precision.HIGHEST)  16.9 us
  transfers between devices with their start and end apart: 2, of which 2 were waited for; matrix products, arithmetic and copies ran while one was open for 1% of the time, Pallas kernels for 0%

commit v1 on v0

--- a/solution.py
+++ b/solution.py
@@ -8,6 +8,18 @@
 K = 131072
 PASSES = 3
 eps = 1e-06
+
+
+def collect(x, axis, dim):
+    ways, here = (lax.axis_size(axis), lax.axis_index(axis))
+    grown, reach = (x, 1)
+    while reach < ways:
+        theirs = lax.ppermute(grown, axis, [(d, d ^ reach) for d in range(ways)])
+        mine_first = jnp.concatenate([grown, theirs], axis=dim)
+        theirs_first = jnp.concatenate([theirs, grown], axis=dim)
+        grown = jnp.where(here & reach == 0, mine_first, theirs_first)
+        reach = 2 * reach
+    return grown
 
 
 def unitize(values):
@@ -30,7 +42,7 @@
     local_s = unitize(student_features)
     unit_t, unit_s = (
         lax.all_gather(local_t, "protos", axis=0, tiled=True),
-        lax.all_gather(local_s, "protos", axis=0, tiled=True),
+        collect(local_s, "protos", 0),
     )
     kernel = jnp.exp(scale * against(unit_t, unit_w))
     powers = jnp.exp(scale * against(unit_s, unit_w))

time: 736 us -> 700 us (0.951)
  blocking collectives: 371 us -> 324 us
  waiting for transfers between devices: 264 us -> 272 us
    all_gather x1 -> x0, blocking collectives: 41.6 us -> none  [on_device(): lax.all_gather(local_s, 'protos', axis=0, tiled=True)]
    psum x3, blocking collectives: 120 us -> 109 us  [on_device(): col_scale = 1.0 / lax.psum(col_part, 'rows')]
  transfers between devices with their start and end apart: 2 -> 7, of which waited for: 2 -> 4; matrix products, arithmetic and copies ran while one was open for 1% -> 9% of each run, Pallas kernels for 0% -> 0%
where the time goes in v1:
time: 700 us
  blocking collectives  324 us (46%)
  waiting for transfers between devices  272 us (39%)
  matrix products  66.1 us (9%)
  between operations  14.2 us (2%)
  other arithmetic  13.2 us (2%)
    reduce_scatter x1, waiting for transfers between devices, on_device(): lax.psum_scatter(feature_term, 'protos', scatter_dimension=0, tiled=True)  214 us
    psum x3, blocking collectives, on_device(): row_whole = lax.psum(row_part, 'protos')  175 us
    psum x3, blocking collectives, on_device(): col_scale = 1.0 / lax.psum(col_part, 'rows')  109 us
    reduce_scatter x1, waiting for transfers between devices, on_device(): lax.psum_scatter(term.reshape(row_groups, block, term.shape[1]), 'rows',...  51.1 us
    all_gather x1, blocking collectives, on_device(): lax.all_gather(local_t, 'protos', axis=0, tiled=True)  39.9 us
    dot_general x3, matrix products, on_device(): row_part = jnp.dot(kernel, col_scale, precision=lax.Precision.HIGHEST)  28.3 us
    dot_general x3, matrix products, on_device(): col_part = jnp.dot(row_scale, kernel, precision=lax.Precision.HIGHEST)  16.9 us
  transfers between devices with their start and end apart: 7, of which 4 were waited for; matrix products, arithmetic and copies ran while one was open for 9% of the time, Pallas kernels for 0%

profile of v1, /device:TPU:1, one launch (start us, length us, event | category | flops | bytes accessed | tf_op | source)
XLA Modules:
  0.0 699.7 jit_solution(5473202222314105378)
XLA Ops:
  7.2 0.0 reduce-scatter.3.cloned.1.call-start
  7.2 0.8 fusion.4
  8.0 0.8 fusion.5
  8.8 2.5 collective-permute-start
  11.3 0.8 fusion.6
  12.1 0.8 fusion.7
  12.9 2.6 fusion.1
  15.5 0.0 copy-start.3
  15.5 39.9 %all_gather.3 = bf16[512,384]{1,0:T(8,128)(2,1)S(1)} all-gather(bf16[16,384]{1,0:T(8,128)(2,1)S(1)} %fusion.7), channel_id=1, replica_groups=mesh['rows'=8,'protos'=32] {'protos'}, dimensions={0}, use_global_device_ids=true | all-gather | bytes 405504 | tf_op jit(solution)/shard_map/all_gather | solution.py:44
  55.4 4.3 multiply_exponential_fusion
  59.8 0.0 copy-start
  59.8 3.2 copy-done
  63.0 4.0 fusion.8
  67.0 0.0 copy-done.3
  67.0 33.2 %psum.50 = f32[4096]{0:T(1024)S(1)} all-reduce(f32[4096]{0:T(1024)S(1)} %bitcast.32), channel_id=1, replica_groups=mesh['rows'=8,'protos'=32] {'rows'}, use_global_device_ids=true, to_apply=%region_5.6 | all-reduce | flops 4096 | bytes 32768 | tf_op jit(solution)/shard_map/psum | solution.py:55
  100.2 9.4 %fusion.16 = f32[1,512]{1,0:T(1,128)S(1)} fusion(f32[512,4096]{1,0:T(8,128)} %copy-done, f32[4096,1]{0,1:T(1,128)S(1)} %bitcast.29), kind=kOutput, calls=%fused_computation.38 | convolution fusion | flops 25165824 | bytes 8407040 | tf_op jit(solution)/shard_map/dot_general | solution.py:56
  109.7 58.6 %psum.51 = f32[512]{0:T(512)S(1)} all-reduce(f32[512]{0:T(512)S(1)} %bitcast.36), channel_id=1, replica_groups=mesh['rows'=8,'protos'=32] {'protos'}, use_global_device_ids=true, to_apply=%region_6.7 | all-reduce | flops 512 | bytes 4096 | tf_op jit(solution)/shard_map/psum | solution.py:58
  168.3 6.3 fusion.17
  174.6 37.4 %psum.52 = f32[4096]{0:T(1024)S(1)} all-reduce(f32[4096]{0:T(1024)S(1)} %bitcast.30), channel_id=1, replica_groups=mesh['rows'=8,'protos'=32] {'rows'}, use_global_device_ids=true, to_apply=%region_7.8 | all-reduce | flops 4096 | bytes 32768 | tf_op jit(solution)/shard_map/psum | solution.py:55
  212.0 9.4 %fusion.18 = f32[1,512]{1,0:T(1,128)S(1)} fusion(f32[512,4096]{1,0:T(8,128)} %copy-done, f32[4096,1]{0,1:T(1,128)S(1)} %bitcast.31), kind=kOutput, calls=%fused_computation.40 | convolution fusion | flops 25165824 | bytes 8407040 | tf_op jit(solution)/shard_map/dot_general | solution.py:56
  221.5 55.8 %psum.53 = f32[512]{0:T(512)S(1)} all-reduce(f32[512]{0:T(512)S(1)} %bitcast.35), channel_id=1, replica_groups=mesh['rows'=8,'protos'=32] {'protos'}, use_global_device_ids=true, to_apply=%region_8.9 | all-reduce | flops 512 | bytes 4096 | tf_op jit(solution)/shard_map/psum | solution.py:60
  277.2 0.0 collective-permute-done
  277.2 0.1 collective-permute-start.1
  277.4 3.5 collective-permute-done.1
  280.9 0.1 collective-permute-start.2
  281.0 0.0 copy-start.1
  281.0 6.5 fusion.19
  287.5 38.6 %psum.54 = f32[4096]{0:T(1024)S(1)} all-reduce(f32[4096]{0:T(1024)S(1)} %bitcast.28), channel_id=1, replica_groups=mesh['rows'=8,'protos'=32] {'rows'}, use_global_device_ids=true, to_apply=%region_9.10 | all-reduce | flops 4096 | bytes 32768 | tf_op jit(solution)/shard_map/psum | solution.py:55
  326.1 0.0 collective-permute-done.2
  326.1 0.1 collective-permute-start.3
  326.3 3.4 collective-permute-done.3
  329.7 1.2 collective-permute-start.4
  330.9 9.4 %fusion.20 = f32[1,512]{1,0:T(1,128)S(1)} fusion(f32[512,4096]{1,0:T(8,128)} %copy-done, f32[4096,1]{0,1:T(1,128)S(1)} %bitcast.27), kind=kOutput, calls=%fused_computation.42 | convolution fusion | flops 25165824 | bytes 8407040 | tf_op jit(solution)/shard_map/dot_general | solution.py:56
  340.4 0.0 collective-permute-done.4
  340.4 0.0 copy-done.1
  340.4 6.0 fusion
  346.3 61.0 %all-reduce = (f32[512]{0:T(512)S(1)}, f32[512]{0:T(512)S(1)}) all-reduce(f32[512]{0:T(512)S(1)} %bitcast.34, f32[512]{0:T(512)S(1)} %get-tuple-element.4), channel_id=1, replica_groups=mesh['rows'=8,'protos'=32] {'protos'}, use_global_device_ids=true, to_apply=%region_10.11 | all-reduce | flops 1024 | bytes 8192 | tf_op jit(solution)/shard_map/psum | solution.py:60
  407.4 0.0 copy-start.4
  407.4 7.3 %subtract_convert_fusion = bf16[512,4096]{1,0:T(8,128)(2,1)S(1)} fusion(f32[512,4096]{1,0:T(8,128)} %copy-done, f32[512,4096]{1,0:T(8,128)} %get-tuple-element.5, f32[4096]{0:T(1024)S(1)} %broadcast_divide_fusion, f32[512]{0:T(512)S(1)} %broadcast_divide_fusion.5, f32[512]{0:T(512)S(1)} %get-tuple-element.3), kind=kLoop, calls=%fused_computation | loop fusion | flops 12582912 | bytes 20992000 | tf_op jit(solution)/shard_map/convert_element_type | solution.py:64
  414.7 0.0 copy-start.2
  414.7 2.0 copy-done.2
  416.7 0.0 copy-done.4
  416.7 3.3 convolution_multiply_fusion.1
  420.0 0.0 reduce-scatter.3.cloned.1.call-update
  420.1 0.0 reduce-scatter.5.cloned.1.call-start
  420.1 7.3 %convolution_multiply_fusion = f32[4096,384]{1,0:T(8,128)} fusion(bf16[512,4096]{1,0:T(8,128)(2,1)} %copy-done.2, bf16[256,384]{1,0:T(8,128)(2,1)} %collective-permute-done.4, bf16[256,384]{1,0:T(8,128)(2,1)S(1)} %maximum_select_fusion.1, pred[]{:T(512)S(6)} %eq.15), kind=kOutput, calls=%fused_computation.8 | convolution fusion | flops 1613955072 | bytes 10878977 | tf_op jit(solution)/shard_map/dot_general | solution.py:71
  427.4 0.0 reduce-scatter.5.cloned.1.call-update
  427.4 214.3 %reduce-scatter.3.cloned.1.call-done = f32[16,384]{1,0:T(8,128)} async-done(((f32[512,384]{1,0:T(8,128)}), f32[16,384]{1,0:T(8,128)}) %reduce-scatter.3.cloned.1.call-update) | async-done | bytes 24592 | tf_op jit(solution)/shard_map/reduce_scatter | solution.py:66
  641.8 51.1 %reduce-scatter.5.cloned.1.call-done = f32[1,512,384]{2,1,0:T(8,128)} async-done(((f32[8,512,384]{2,1,0:T(8,128)}), f32[1,512,384]{2,1,0:T(8,128)}) %reduce-scatter.5.cloned.1.call-update) | async-done | bytes 786448 | tf_op jit(solution)/shard_map/reduce_scatter | solution.py:74
  (13 shorter events, 0.1 us)
Async XLA Ops:
  7.2 634.6 %reduce-scatter.3.cloned.1.call-start = ((), (), s32[]{:S(2)}) async-start(), calls=%async_computation.2 | async-start | bytes 811008 | tf_op jit(solution)/shard_map/reduce_scatter | solution.py:66
  8.8 268.4 %collective-permute-start = (bf16[16,384]{1,0:T(8,128)(2,1)S(1)}, bf16[16,384]{1,0:T(8,128)(2,1)S(1)}, u32[]{:S(2)}, u32[]{:S(2)}) collective-permute-start(bf16[16,384]{1,0:T(8,128)(2,1)S(1)} %fusion.5), channel_id=1, source_target_pairs={{0,1},{1,0},{2,3},{3,2},{4,5},{5,4},{6,7},{7,6},{8,9},{9,8},{10,11... | collective-permute-start | bytes 36872 | tf_op jit(solution)/shard_map/ppermute | solution.py:17
  15.5 51.5 %copy-start.3 = (f32[4096]{0:T(1024)}, f32[4096]{0:T(1024)S(1)}, u32[]{:S(2)}) copy-start(f32[4096]{0:T(1024)S(1)} %add_rsqrt_fusion) | copy-start | bytes 49156
  59.8 3.2 copy-start
  277.2 3.7 collective-permute-start.1
  280.9 45.2 %collective-permute-start.2 = (bf16[64,384]{1,0:T(8,128)(2,1)S(1)}, bf16[64,384]{1,0:T(8,128)(2,1)S(1)}, u32[]{:S(2)}, u32[]{:S(2)}) collective-permute-start(bf16[64,384]{1,0:T(8,128)(2,1)S(1)} %maximum_select_fusion.5), channel_id=1, source_target_pairs={{0,4},{1,5},{2,6},{3,7},{4,0},{5,1},{6,2},{7,3},{8,12},{9,13},{10,... | collective-permute-start | bytes 147464 | tf_op jit(solution)/shard_map/ppermute | solution.py:17
  281.0 59.4 %copy-start.1 = (bf16[4096,384]{1,0:T(8,128)(2,1)S(1)}, bf16[4096,384]{1,0:T(8,128)(2,1)}, u32[]{:S(2)}) copy-start(bf16[4096,384]{1,0:T(8,128)(2,1)} %param.5) | copy-start | bytes 9437188
  326.1 3.6 collective-permute-start.3
  329.7 10.6 %collective-permute-start.4 = (bf16[256,384]{1,0:T(8,128)(2,1)S(1)}, bf16[256,384]{1,0:T(8,128)(2,1)}, u32[]{:S(2)}, u32[]{:S(2)}) collective-permute-start(bf16[256,384]{1,0:T(8,128)(2,1)S(1)} %maximum_select_fusion.1), channel_id=1, source_target_pairs={{0,16},{1,17},{2,18},{3,19},{4,20},{5,21},{6,22},{7,23},{8,24},{9,... | collective-permute-start | bytes 589832 | tf_op jit(solution)/shard_map/ppermute | solution.py:17
  407.4 9.3 %copy-start.4 = (f32[4096]{0:T(1024)S(1)}, f32[4096]{0:T(1024)}, u32[]{:S(2)}) copy-start(f32[4096]{0:T(1024)} %copy-done.3) | copy-start | bytes 49156
  414.7 2.0 copy-start.2
  420.1 272.8 %reduce-scatter.5.cloned.1.call-start = ((), (), s32[]{:S(2)}) async-start(), calls=%async_computation.3 | async-start | bytes 7077888 | tf_op jit(solution)/shard_map/reduce_scatter | solution.py:74
Sparse Core Ops, SparseCore 0:
  420.2 221.5 reduce-scatter.2
  644.9 47.8 reduce-scatter.4
